TPU v7x, 256 devices: a whole 4x4x8 slice. The times are simulated.
256 devices in a mesh: wide: 32 (over y, x, core), narrow: 8 (over z).
Axes of the slice: x: 4, y: 4, z: 8, core: 2. Of those that a mesh axis runs over, the one named last changes fastest.
Arguments:
- amplitudes: bfloat16 [1024, 16, 4096], P('wide', None, 'narrow'), may hold values from -6 to 6
- amp_tiles: int32 [32, 16], replicated, may hold values from 0 to 31, all different within a row
- integrals: bfloat16 [32, 2, 4096, 4096], P('wide', None, None, 'narrow'), may hold values from -0.09375 to 0.09375
- cd_tiles: int32 [32, 2], replicated, may hold values from 0 to 31, all different within a row
- q_owner: int32 [32], replicated, may hold values from 0 to 31, each once
Outputs:
- residual: bfloat16 [1024, 32, 4096], P('wide', None, 'narrow')
Inputs may be any that keep to these rules, and one draw needn't show every extreme that they name: `amp_tiles`: within a row, the 16 tiles are different. `cd_tiles`: within a row, the 2 tiles are different; every tile is named by some row. `q_owner`: each owner index appears once.
All inputs are finite; a program needn't handle non-finite values.
Results may differ from a plain program's by a relative error of at most 0.017.
Values may be sent and summed in bfloat16 or wider, within the bound.
A program may use at most 64 MiB of HBM per device.

v0:
```python
import jax
import jax.numpy as jnp
from jax import lax
from jax.sharding import PartitionSpec as P


def on_device(amplitudes, amp_tiles, integrals, cd_tiles, q_owner):
    my_index = lax.axis_index("wide")
    blocks = lax.axis_size("wide")
    rows_dev = amplitudes.shape[0]
    local_ints = integrals[0]
    tile_ids = jnp.arange(q_owner.shape[0], dtype=jnp.int32)
    holder = (q_owner[None, :] == jnp.arange(blocks, dtype=jnp.int32)[:, None]).astype(jnp.int32)
    owned_tile = jnp.sum(holder * tile_ids[None, :], axis=1)
    wanted = cd_tiles[owned_tile]
    my_wanted = wanted[my_index]
    segment = lax.all_gather(amplitudes, "wide", axis=0, tiled=True)
    length = segment.shape[0]
    source = jnp.arange(length, dtype=jnp.int32) // rows_dev
    tile_list = amp_tiles[source]
    picker = (tile_list[:, :, None] == my_wanted[None, None, :]).astype(jnp.bfloat16)
    chosen = jnp.einsum("rtk,rtc->rkc", picker, segment, preferred_element_type=jnp.float32).astype(
        jnp.bfloat16
    )
    partial_value = jnp.einsum(
        "rkc,kpc->rp", chosen, local_ints, preferred_element_type=jnp.float32
    )
    shares = lax.psum_scatter(
        partial_value.astype(jnp.bfloat16), "narrow", scatter_dimension=1, tiled=True
    )
    returned = lax.all_to_all(
        shares.reshape(blocks, rows_dev, shares.shape[1]),
        "wide",
        split_axis=0,
        concat_axis=0,
        tiled=True,
    )
    result = jnp.take(returned, q_owner, axis=0)
    return jnp.transpose(result, (1, 0, 2))


def solution(mesh):
    placed = (P("wide", None, "narrow"), P(), P("wide", None, None, "narrow"), P(), P())
    return jax.shard_map(
        on_device, mesh=mesh, in_specs=placed, out_specs=P("wide", None, "narrow"), check_vma=False
    )
```

profile of v0, /device:TPU:1, one launch (start us, length us, event | category | flops | bytes accessed | tf_op | source)
XLA Modules:
  0.0 242.8 jit_solution(6019152147181182622)
XLA Ops:
  6.5 0.0 all-gather.2.cloned.1.call-start
  6.5 0.7 all-gather.2.cloned.1.call-update
  7.3 0.0 reduce-scatter.2.cloned.1.call-start
  7.3 0.8 copy.16
  8.1 0.8 copy.15
  8.8 0.8 select_reduce_fusion
  9.6 0.6 gather_fusion.1
  10.2 2.8 %gather_fusion = s32[1024,16]{1,0:T(8,128)S(1)} fusion(s32[32,16]{1,0:T(8,128)S(1)} %copy.15, s32[1024]{0:T(1024)S(1)} %broadcast_clamp_fusion), kind=kCustom, calls=%fused_computation | custom fusion | bytes 135168 | tf_op jit(solution)/shard_map/gather | solution.py:20
  13.1 78.6 %all-gather.2.cloned.1.call-done = bf16[1024,16,512]{2,1,0:T(8,128)(2,1)} async-done(((bf16[32,16,512]{2,1,0:T(8,128)(2,1)}), bf16[1024,16,512]{2,1,0:T(8,128)(2,1)}) %all-gather.2.cloned.1.call-update) | async-done | bytes 16777232 | tf_op jit(solution)/shard_map/all_gather | solution.py:17
  91.7 8.6 %convolution_convert_fusion = bf16[1024,2,512]{2,1,0:T(2,128)(2,1)S(1)} fusion(bf16[1024,16,512]{2,1,0:T(8,128)(2,1)} %all-gather.2.cloned.1.call-done, s32[1024,16]{1,0:T(8,128)S(1)} %gather_fusion, s32[2]{0:T(128)S(1)} %dynamic-slice_bitcast_fusion), kind=kOutput, calls=%fused_computation.5 | convolution fusion | flops 34635776 | bytes 18939912 | tf_op jit(solution)/shard_map/rtk,rtc->rkc/dot_general | solution.py:22
  100.3 14.4 %bitcast_convert_fusion = bf16[1024,4096]{1,0:T(8,128)(2,1)} fusion(bf16[1,2,4096,512]{3,2,1,0:T(8,128)(2,1)} %param.7, bf16[1024,2,512]{2,1,0:T(2,128)(2,1)S(1)} %convolution_convert_fusion), kind=kOutput, calls=%fused_computation.3 | convolution fusion | flops 8594128896 | bytes 18874368 | tf_op jit(solution)/shard_map/rkc,kpc->rp/dot_general | solution.py:25
  114.6 0.0 copy-start
  114.7 0.0 reduce-scatter.2.cloned.1.call-update
  114.7 94.2 %reduce-scatter.2.cloned.1.call-done = bf16[1024,512]{1,0:T(8,128)(2,1)} async-done(((bf16[1024,4096]{1,0:T(8,128)(2,1)}), bf16[1024,512]{1,0:T(8,128)(2,1)}) %reduce-scatter.2.cloned.1.call-update) | async-done | bytes 1048592 | tf_op jit(solution)/shard_map/reduce_scatter | solution.py:28
  208.9 7.5 %all-to-all-start = ((bf16[32,32,512]{2,1,0:T(8,128)(2,1)}), bf16[32,32,512]{2,1,0:T(8,128)(2,1)S(1)}, u32[]{:S(2)}, u32[]{:S(2)}) async-start(bf16[32,32,512]{2,1,0:T(8,128)(2,1)} %bitcast.16), calls=%async_computation.1 | async-start | bytes 2097152 | tf_op jit(solution)/shard_map/all_to_all | solution.py:31
  216.4 0.0 copy-done
  216.5 17.1 %all-to-all-done = bf16[32,32,512]{2,1,0:T(8,128)(2,1)S(1)} async-done(((bf16[32,32,512]{2,1,0:T(8,128)(2,1)}), bf16[32,32,512]{2,1,0:T(8,128)(2,1)S(1)}, u32[]{:S(2)}, u32[]{:S(2)}) %all-to-all-start) | async-done | bytes 1048608 | tf_op jit(solution)/shard_map/all_to_all | solution.py:31
  233.6 0.6 gather_fusion.2
  234.2 0.2 select_bitcast_fusion
  234.4 1.5 copy.18
  (8 shorter events, 0.1 us)
Async XLA Ops:
  6.5 85.1 %all-gather.2.cloned.1.call-start = ((), (), s32[]{:S(2)}) async-start(), calls=%async_computation.2 | async-start | bytes 17301504 | tf_op jit(solution)/shard_map/all_gather | solution.py:17
  7.3 201.7 %reduce-scatter.2.cloned.1.call-start = ((), (), s32[]{:S(2)}) async-start(), calls=%async_computation.3 | async-start | bytes 9437184 | tf_op jit(solution)/shard_map/reduce_scatter | solution.py:28
  114.6 101.8 %copy-start = (s32[32]{0:T(128)S(1)}, s32[32]{0:T(128)}, u32[]{:S(2)}) copy-start(s32[32]{0:T(128)} %param.9) | copy-start | bytes 388
  208.9 24.7 %all-to-all-start = ((bf16[32,32,512]{2,1,0:T(8,128)(2,1)}), bf16[32,32,512]{2,1,0:T(8,128)(2,1)S(1)}, u32[]{:S(2)}, u32[]{:S(2)}) async-start(bf16[32,32,512]{2,1,0:T(8,128)(2,1)} %bitcast.16), calls=%async_computation.1 | async-start | bytes 2097152 | tf_op jit(solution)/shard_map/all_to_all | solution.py:31
Sparse Core Ops, SparseCore 0:
  9.9 81.7 all-gather.1
  114.8 94.0 reduce-scatter.1
where the time goes:
time: 243 us
  waiting for transfers between devices  191 us (79%)
  matrix products  23 us (9%)
  between operations  13.5 us (6%)
  starting transfers between devices  7.52 us (3%)
  local copies, waits for them, and re-layouts  7.09 us (3%)
    reduce_scatter x1, waiting for transfers between devices, on_device(): lax.psum_scatter(partial_value.astype(jnp.bfloat16), 'narrow', scatter_di...  94.2 us
    all_gather x1, waiting for transfers between devices, on_device(): segment = lax.all_gather(amplitudes, 'wide', axis=0, tiled=True)  78.6 us
    all_to_all x1, waiting for transfers between devices, on_device(): lax.all_to_all(shares.reshape(blocks, rows_dev, shares.shape[1]), 'wide',...  17.1 us
    dot_general x1, matrix products, on_device(): jnp.einsum('rkc,kpc->rp', chosen, local_ints, preferred_element_type=jnp....  14.4 us
    dot_general x1, matrix products, on_device(): jnp.einsum('rtk,rtc->rkc', picker, segment, preferred_element_type=jnp.fl...  8.62 us
    all_to_all x1, starting transfers between devices, on_device(): lax.all_to_all(shares.reshape(blocks, rows_dev, shares.shape[1]), 'wide',...  7.48 us
  transfers between devices with their start and end apart: 3, of which 3 were waited for; matrix products, arithmetic and copies ran while one was open for 2% of the time, Pallas kernels for 0%

commit v1 on v0

--- a/solution.py
+++ b/solution.py
@@ -5,6 +5,13 @@
 
 
 def on_device(amplitudes, amp_tiles, integrals, cd_tiles, q_owner):
+
+    def _track_slices(xx, peer_axis="wide"):
+        right_arr = jnp.concatenate([xx for _ in range(lax.axis_size(peer_axis))], 0)
+        return lax.all_to_all(
+            right_arr, axis_name=peer_axis, split_axis=0, concat_axis=0, tiled=True
+        )
+
     my_index = lax.axis_index("wide")
     blocks = lax.axis_size("wide")
     rows_dev = amplitudes.shape[0]
@@ -14,7 +21,7 @@
     owned_tile = jnp.sum(holder * tile_ids[None, :], axis=1)
     wanted = cd_tiles[owned_tile]
     my_wanted = wanted[my_index]
-    segment = lax.all_gather(amplitudes, "wide", axis=0, tiled=True)
+    segment = _track_slices(amplitudes)
     length = segment.shape[0]
     source = jnp.arange(length, dtype=jnp.int32) // rows_dev
     tile_list = amp_tiles[source]

time: 243 us -> 423 us (1.74)
  waiting for transfers between devices: 191 us -> 319 us
  local copies, waits for them, and re-layouts: 7.09 us -> 50.4 us
  starting transfers between devices: 7.52 us -> 16.3 us
    all_to_all x0 -> x1, waiting for transfers between devices: none -> 197 us  [_track_slices(): lax.all_to_all(right_arr, axis_name=peer_axis, split_axis=0, concat_axis=...]
    all_gather x1 -> x0, waiting for transfers between devices: 78.6 us -> none  [on_device(): segment = lax.all_gather(amplitudes, 'wide', axis=0, tiled=True)]
    unnamed x4 -> x41, local copies, waits for them, and re-layouts: 1.53 us -> 42.9 us
    reduce_scatter x1, waiting for transfers between devices: 94.2 us -> 104 us  [on_device(): lax.psum_scatter(partial_value.astype(jnp.bfloat16), 'narrow', scatter_di...]
    all_to_all x0 -> x1, starting transfers between devices: none -> 8.77 us  [_track_slices(): lax.all_to_all(right_arr, axis_name=peer_axis, split_axis=0, concat_axis=...]
  transfers between devices with their start and end apart: 3 -> 3, of which waited for: 3 -> 3; matrix products, arithmetic and copies ran while one was open for 2% -> 1% of each run, Pallas kernels for 0% -> 0%
where the time goes in v1:
time: 423 us; the launch traced here: 422 us
  waiting for transfers between devices  319 us (75%)
  local copies, waits for them, and re-layouts  50.4 us (12%)
  matrix products  23 us (5%)
  starting transfers between devices  16.3 us (4%)
  between operations  13.5 us (3%)
    all_to_all x1, waiting for transfers between devices, _track_slices(): lax.all_to_all(right_arr, axis_name=peer_axis, split_axis=0, concat_axis=...  197 us
    reduce_scatter x1, waiting for transfers between devices, on_device(): lax.psum_scatter(partial_value.astype(jnp.bfloat16), 'narrow', scatter_di...  104 us
    unnamed x41, local copies, waits for them, and re-layouts  42.9 us
    all_to_all x1, waiting for transfers between devices, on_device(): lax.all_to_all(shares.reshape(blocks, rows_dev, shares.shape[1]), 'wide',...  17.1 us
    dot_general x1, matrix products, on_device(): jnp.einsum('rkc,kpc->rp', chosen, local_ints, preferred_element_type=jnp....  14.4 us
    all_to_all x1, starting transfers between devices, _track_slices(): lax.all_to_all(right_arr, axis_name=peer_axis, split_axis=0, concat_axis=...  8.77 us
    dot_general x1, matrix products, on_device(): jnp.einsum('rtk,rtc->rkc', picker, segment, preferred_element_type=jnp.fl...  8.64 us
  transfers between devices with their start and end apart: 3, of which 3 were waited for; matrix products, arithmetic and copies ran while one was open for 1% of the time, Pallas kernels for 0%

profile of v1, /device:TPU:1, one launch (start us, length us, event | category | flops | bytes accessed | tf_op | source)
XLA Modules:
  0.0 422.2 jit_solution(11341409414122779540)
XLA Ops:
  6.5 0.0 copy-start
  6.5 1.9 constant_dynamic-update-slice_fusion.31
  8.5 1.9 constant_dynamic-update-slice_fusion.30
  10.3 1.9 constant_dynamic-update-slice_fusion.29
  12.2 1.9 constant_dynamic-update-slice_fusion.28
  14.1 1.9 constant_dynamic-update-slice_fusion.27
  16.0 1.9 constant_dynamic-update-slice_fusion.26
  17.9 1.9 constant_dynamic-update-slice_fusion.25
  19.7 1.9 constant_dynamic-update-slice_fusion.24
  21.6 1.9 constant_dynamic-update-slice_fusion.23
  23.5 1.9 constant_dynamic-update-slice_fusion.22
  25.3 1.9 constant_dynamic-update-slice_fusion.21
  27.2 1.9 constant_dynamic-update-slice_fusion.20
  29.1 1.9 constant_dynamic-update-slice_fusion.19
  31.0 1.9 constant_dynamic-update-slice_fusion.18
  32.9 1.8 constant_dynamic-update-slice_fusion.17
  34.7 1.9 constant_dynamic-update-slice_fusion.16
  36.6 0.0 copy-done
  36.6 0.9 constant_dynamic-update-slice_fusion.15
  37.5 0.9 constant_dynamic-update-slice_fusion.14
  38.4 0.8 constant_dynamic-update-slice_fusion.13
  39.2 0.8 constant_dynamic-update-slice_fusion.12
  40.0 0.9 constant_dynamic-update-slice_fusion.11
  40.9 0.8 constant_dynamic-update-slice_fusion.10
  41.7 0.8 constant_dynamic-update-slice_fusion.9
  42.5 0.8 constant_dynamic-update-slice_fusion.8
  43.4 0.8 constant_dynamic-update-slice_fusion.7
  44.2 0.8 constant_dynamic-update-slice_fusion.6
  45.1 0.8 constant_dynamic-update-slice_fusion.5
  45.9 0.8 constant_dynamic-update-slice_fusion.4
  46.7 0.9 constant_dynamic-update-slice_fusion.3
  47.6 0.9 constant_dynamic-update-slice_fusion.2
  48.4 0.8 constant_dynamic-update-slice_fusion.1
  49.3 0.8 constant_dynamic-update-slice_fusion
  50.1 0.0 copy-start.2
  50.1 0.0 copy-start.1
  50.1 0.0 copy-start.3
  50.1 8.8 %all-to-all-start = ((bf16[1024,16,512]{2,1,0:T(8,128)(2,1)}), bf16[1024,16,512]{2,1,0:T(8,128)(2,1)}, u32[]{:S(2)}, u32[]{:S(2)}) async-start(bf16[1024,16,512]{2,1,0:T(8,128)(2,1)} %constant_dynamic-update-slice_fusion), calls=%async_computation | async-start | bytes 33554432 | tf_op jit(solution)/shard_map/all_to_all | solution.py:11
  58.9 0.0 reduce-scatter.2.cloned.1.call-start
  58.9 0.0 copy-done.2
  59.0 0.1 copy.13
  59.0 0.0 copy-done.1
  59.0 0.1 copy.11
  59.1 0.0 copy-done.3
  59.1 0.1 select_reduce_fusion
  59.3 2.8 gather_fusion
  62.1 0.2 copy.12
  62.3 0.6 gather_fusion.1
  62.9 0.1 broadcast_compare_fusion
  63.0 0.9 copy.14
  63.9 196.9 %all-to-all-done = bf16[1024,16,512]{2,1,0:T(8,128)(2,1)} async-done(((bf16[1024,16,512]{2,1,0:T(8,128)(2,1)}), bf16[1024,16,512]{2,1,0:T(8,128)(2,1)}, u32[]{:S(2)}, u32[]{:S(2)}) %all-to-all-start) | async-done | bytes 16777248 | tf_op jit(solution)/shard_map/all_to_all | solution.py:11
  260.8 8.6 %convolution_convert_fusion = bf16[1024,2,512]{2,1,0:T(2,128)(2,1)S(1)} fusion(pred[1024,16,2]{1,2,0:T(4,128)(4,1)S(1)} %copy.14, bf16[1024,16,512]{2,1,0:T(8,128)(2,1)} %all-to-all-done), kind=kOutput, calls=%fused_computation.5 | convolution fusion | flops 34603008 | bytes 18907136 | tf_op jit(solution)/shard_map/rtk,rtc->rkc/dot_general | solution.py:29
  269.5 14.4 %bitcast_convert_fusion = bf16[1024,4096]{1,0:T(8,128)(2,1)} fusion(bf16[1,2,4096,512]{3,2,1,0:T(8,128)(2,1)} %param.7, bf16[1024,2,512]{2,1,0:T(2,128)(2,1)S(1)} %convolution_convert_fusion), kind=kOutput, calls=%fused_computation.3 | convolution fusion | flops 8594128896 | bytes 18874368 | tf_op jit(solution)/shard_map/rkc,kpc->rp/dot_general | solution.py:32
  283.8 0.0 reduce-scatter.2.cloned.1.call-update
  283.9 104.5 %reduce-scatter.2.cloned.1.call-done = bf16[1024,512]{1,0:T(8,128)(2,1)} async-done(((bf16[1024,4096]{1,0:T(8,128)(2,1)}), bf16[1024,512]{1,0:T(8,128)(2,1)}) %reduce-scatter.2.cloned.1.call-update) | async-done | bytes 1048592 | tf_op jit(solution)/shard_map/reduce_scatter | solution.py:35
  388.3 7.5 %all-to-all-start.1 = ((bf16[32,32,512]{2,1,0:T(8,128)(2,1)}), bf16[32,32,512]{2,1,0:T(8,128)(2,1)S(1)}, u32[]{:S(2)}, u32[]{:S(2)}) async-start(bf16[32,32,512]{2,1,0:T(8,128)(2,1)} %bitcast.17), calls=%async_computation.2 | async-start | bytes 2097152 | tf_op jit(solution)/shard_map/all_to_all | solution.py:38
  395.9 17.1 %all-to-all-done.1 = bf16[32,32,512]{2,1,0:T(8,128)(2,1)S(1)} async-done(((bf16[32,32,512]{2,1,0:T(8,128)(2,1)}), bf16[32,32,512]{2,1,0:T(8,128)(2,1)S(1)}, u32[]{:S(2)}, u32[]{:S(2)}) %all-to-all-start.1) | async-done | bytes 1048608 | tf_op jit(solution)/shard_map/all_to_all | solution.py:38
  413.0 0.6 gather_fusion.2
  413.6 0.2 select_bitcast_fusion
  413.8 1.5 copy.16
  (7 shorter events, 0.1 us)
Async XLA Ops:
  6.5 30.1 %copy-start = (bf16[32,16,512]{2,1,0:T(8,128)(2,1)S(1)}, bf16[32,16,512]{2,1,0:T(8,128)(2,1)}, u32[]{:S(2)}) copy-start(bf16[32,16,512]{2,1,0:T(8,128)(2,1)} %param.5) | copy-start | bytes 1572868
  50.1 8.8 %copy-start.2 = (s32[32,2]{0,1:T(2,128)S(1)}, s32[32,2]{0,1:T(2,128)}, u32[]{:S(2)}) copy-start(s32[32,2]{0,1:T(2,128)} %param.8) | copy-start | bytes 772
  50.1 8.9 %copy-start.1 = (s32[32,16]{0,1:T(8,128)S(1)}, s32[32,16]{0,1:T(8,128)}, u32[]{:S(2)}) copy-start(s32[32,16]{0,1:T(8,128)} %param.6) | copy-start | bytes 6148
  50.1 9.0 %copy-start.3 = (s32[32]{0:T(128)S(1)}, s32[32]{0:T(128)}, u32[]{:S(2)}) copy-start(s32[32]{0:T(128)} %param.9) | copy-start | bytes 388
  50.1 210.7 %all-to-all-start = ((bf16[1024,16,512]{2,1,0:T(8,128)(2,1)}), bf16[1024,16,512]{2,1,0:T(8,128)(2,1)}, u32[]{:S(2)}, u32[]{:S(2)}) async-start(bf16[1024,16,512]{2,1,0:T(8,128)(2,1)} %constant_dynamic-update-slice_fusion), calls=%async_computation | async-start | bytes 33554432 | tf_op jit(solution)/shard_map/all_to_all | solution.py:11
  58.9 329.5 %reduce-scatter.2.cloned.1.call-start = ((), (), s32[]{:S(2)}) async-start(), calls=%async_computation.3 | async-start | bytes 9437184 | tf_op jit(solution)/shard_map/reduce_scatter | solution.py:35
  388.3 24.7 %all-to-all-start.1 = ((bf16[32,32,512]{2,1,0:T(8,128)(2,1)}), bf16[32,32,512]{2,1,0:T(8,128)(2,1)S(1)}, u32[]{:S(2)}, u32[]{:S(2)}) async-start(bf16[32,32,512]{2,1,0:T(8,128)(2,1)} %bitcast.17), calls=%async_computation.2 | async-start | bytes 2097152 | tf_op jit(solution)/shard_map/all_to_all | solution.py:38
Sparse Core Ops, SparseCore 0:
  284.0 104.3 reduce-scatter.1
